TPU v7x, 32 devices: a whole 2x2x4 slice. The times are simulated.
32 devices in a mesh: blk: 8 (over z, x), grp: 4 (over y, core).
Axes of the slice: x: 2, y: 2, z: 4, core: 2. Of those that a mesh axis runs over, the one named last changes fastest.
Arguments:
- queries: bfloat16 [16384, 512], P(('blk', 'grp')), may hold values from -64 to 64
- keys: bfloat16 [16384, 128], P(('blk', 'grp')), may hold values from -8 to 8
- values: bfloat16 [16384, 128], P(('blk', 'grp')), may hold values from -6 to 6
- selected: int32 [32, 16], replicated, may hold values from 0 to 255, as said below
- key_in: bfloat16 [4096, 256], replicated, may hold values from -0.09375 to 0.09375
- key_out: bfloat16 [256, 128], replicated, may hold values from -0.375 to 0.375
- value_in: bfloat16 [4096, 256], replicated, may hold values from -0.09375 to 0.09375
- value_out: bfloat16 [256, 128], replicated, may hold values from -0.375 to 0.375
- positions: bfloat16 [2, 32, 128], replicated, may hold values from -5 to 5
- gate_weight: bfloat16 [512, 12], replicated, may hold values from -0.25 to 0.25
Outputs:
- attended: bfloat16 [16384, 512], P(('blk', 'grp'))
Inputs may be any that keep to these rules, and one draw needn't show every extreme that they name: `selected`: row d lists 16 different fine blocks. Write r = 32 and b = d // 4. Entry 0 is the first fine block of group d's own tokens. Every listed block j with j // r different from b has j // r < b, and no two listed blocks share a value of j // r other than b. Blocks with j // r == b may lie after group d's tokens.
All inputs are finite; a program needn't handle non-finite values.
Results may differ from a plain program's by a relative error of at most 0.004.
Values may be sent and summed in bfloat16 or wider, within the bound.
A program may use at most 64 MiB of HBM per device.

v0:
```python
import jax
import jax.numpy as jnp
from jax import lax
from jax.sharding import PartitionSpec as P

HEAD_DIM = 128
HEADS = 4
CMP_BLOCK = 32
SEL_BLOCK = 64
TOPN = 16
WINDOW = 512


NEG = -1e30


def from_behind(block, axis, distance):
    devices = range(lax.axis_size(axis))
    route = [(i - distance, i) for i in devices if i - distance in devices]
    return lax.ppermute(block, axis, route)


def compress(tokens, shift, w_in, w_out):
    count = tokens.shape[0] // CMP_BLOCK
    mixed = (
        tokens.astype(jnp.float32).reshape(count, CMP_BLOCK, HEAD_DIM)
        + shift.astype(jnp.float32)[None]
    )
    flat = mixed.astype(jnp.bfloat16).reshape(count, CMP_BLOCK * HEAD_DIM)
    hidden = jax.nn.silu(jnp.dot(flat, w_in, preferred_element_type=jnp.float32)).astype(
        jnp.bfloat16
    )
    return jnp.dot(hidden, w_out, preferred_element_type=jnp.float32).astype(jnp.bfloat16)


def attend(query_rows, query_pos, key_rows, value_rows, key_pos, span):
    scale = HEAD_DIM ** (-0.5)
    scores = (
        jnp.einsum("qhd,kd->qhk", query_rows, key_rows, preferred_element_type=jnp.float32) * scale
    )
    allowed = (
        (key_pos[None, :] <= query_pos[:, None])
        & (key_pos[None, :] > query_pos[:, None] - span)
        & (key_pos[None, :] >= 0)
    )
    scores = jnp.where(allowed[:, None, :], scores, NEG)
    top = jnp.max(scores, axis=2, keepdims=True)
    weights = jnp.exp(scores - top)
    total = jnp.sum(weights, axis=2)
    mixed = jnp.einsum(
        "qhk,kd->qhd", weights.astype(jnp.bfloat16), value_rows, preferred_element_type=jnp.float32
    )
    return mixed / total[..., None]


def make_fold(query_heads, query_pos):
    scale = HEAD_DIM ** (-0.5)
    toks = query_heads.shape[0]

    def fold(carry, piece, start):
        best, total, accum = carry
        piece_keys, piece_values = piece
        count = piece_keys.shape[0]
        key_end = jnp.arange(count, dtype=jnp.int32) * CMP_BLOCK + (CMP_BLOCK - 1)
        block_rows = toks
        while (
            block_rows > 32 and block_rows % 2 == 0 and (HEADS * block_rows * count * 4 > 1 << 24)
        ):
            block_rows = block_rows // 2
        steps = toks // block_rows

        def one(items):
            rows, pos, old_best, old_total, old_accum = items
            scores = (
                jnp.einsum("qhd,kd->qhk", rows, piece_keys, preferred_element_type=jnp.float32)
                * scale
            )
            scores = jnp.where((key_end[None, :] <= pos[:, None])[:, None, :], scores, NEG)
            new_best = jnp.maximum(old_best, jnp.max(scores, axis=2))
            weights = jnp.exp(scores - new_best[..., None])
            factor = jnp.exp(old_best - new_best)
            new_total = old_total * factor + jnp.sum(weights, axis=2)
            product = jnp.einsum(
                "qhk,kd->qhd",
                weights.astype(jnp.bfloat16),
                piece_values,
                preferred_element_type=jnp.float32,
            )
            return (new_best, new_total, old_accum * factor[..., None] + product)

        items = (
            query_heads.reshape(steps, block_rows, HEADS, HEAD_DIM),
            query_pos.reshape(steps, block_rows),
            best.reshape(steps, block_rows, HEADS),
            total.reshape(steps, block_rows, HEADS),
            accum.reshape(steps, block_rows, HEADS, HEAD_DIM),
        )
        new_best, new_total, new_accum = lax.map(one, items)
        return (
            new_best.reshape(toks, HEADS),
            new_total.reshape(toks, HEADS),
            new_accum.reshape(toks, HEADS, HEAD_DIM),
        )

    return fold


def per_device(
    queries, keys, values, selected, key_in, key_out, value_in, value_out, positions, gate_weight
):
    stretches = lax.axis_size("blk")
    group_size = lax.axis_size("grp")
    stretch = lax.axis_index("blk")
    column = lax.axis_index("grp")
    toks = queries.shape[0]
    seq_len = stretches * group_size * toks
    position = stretch * group_size + column
    query_pos = position * toks + jnp.arange(toks, dtype=jnp.int32)
    query_heads = queries.reshape(toks, HEADS, HEAD_DIM)
    row_keys, row_values = (
        lax.all_gather(keys, "grp", axis=0, tiled=True),
        lax.all_gather(values, "grp", axis=0, tiled=True),
    )
    fold = make_fold(query_heads, query_pos)
    start_state = (
        jnp.zeros((toks, HEADS), jnp.float32),
        jnp.ones((toks, HEADS), jnp.float32),
        jnp.zeros((toks, HEADS, HEAD_DIM), jnp.float32),
    )
    packed = (
        compress(row_keys, positions[0], key_in, key_out),
        compress(row_values, positions[1], value_in, value_out),
    )
    best, total, accum = fold(
        start_state,
        (
            lax.all_gather(packed[0], "blk", axis=0, tiled=True),
            lax.all_gather(packed[1], "blk", axis=0, tiled=True),
        ),
        jnp.int32(0),
    )
    coarse = accum / total[..., None]
    per_row = group_size * toks // SEL_BLOCK
    row_blocks = jnp.concatenate([row_keys, row_values], axis=1).reshape(
        per_row, SEL_BLOCK, 2 * HEAD_DIM
    )
    requests = jnp.take(selected.reshape(stretches, group_size, TOPN), column, axis=1)
    targets = jnp.arange(stretches, dtype=jnp.int32)
    match = (requests // per_row == stretch) & (targets[:, None] != stretch)
    picked = jnp.sum(jnp.where(match, requests % per_row, 0), axis=1)
    outgoing = jnp.take(row_blocks, picked, axis=0)
    incoming = lax.all_to_all(outgoing, "blk", split_axis=0, concat_axis=0, tiled=True)
    mine = lax.dynamic_index_in_dim(selected, position, 0, keepdims=False)
    owners = mine // per_row
    nearby = jnp.take(row_blocks, mine % per_row, axis=0)
    remote = jnp.take(incoming, owners, axis=0)
    fine_rows = jnp.where((owners == stretch)[:, None, None], nearby, remote).reshape(
        TOPN * SEL_BLOCK, 2 * HEAD_DIM
    )
    fine_keys = fine_rows[:, :HEAD_DIM]
    fine_values = fine_rows[:, HEAD_DIM:]
    fine_pos = (
        mine[:, None] * SEL_BLOCK + jnp.arange(SEL_BLOCK, dtype=jnp.int32)[None, :]
    ).reshape(-1)
    reach = (WINDOW + toks - 1) // toks
    moved_keys, moved_values = from_behind((keys, values), ("blk", "grp"), 1)
    key_parts = [moved_keys]
    value_parts = [moved_values]
    wide_keys = jnp.concatenate(key_parts + [keys], axis=0)
    wide_values = jnp.concatenate(value_parts + [values], axis=0)
    wide_pos = position * toks - reach * toks + jnp.arange((reach + 1) * toks, dtype=jnp.int32)
    block_rows = min(toks, 128)
    steps = toks // block_rows

    def both_blocks(index):
        first = index * block_rows
        rows = lax.dynamic_slice_in_dim(query_heads, first, block_rows, 0)
        pos = lax.dynamic_slice_in_dim(query_pos, first, block_rows, 0)
        fine_part = attend(rows, pos, fine_keys, fine_values, fine_pos, seq_len + 1)
        key_start = reach * toks + first - WINDOW
        near_keys = lax.dynamic_slice_in_dim(wide_keys, key_start, block_rows + WINDOW, 0)
        near_values = lax.dynamic_slice_in_dim(wide_values, key_start, block_rows + WINDOW, 0)
        near_pos = lax.dynamic_slice_in_dim(wide_pos, key_start, block_rows + WINDOW, 0)
        local_part = attend(rows, pos, near_keys, near_values, near_pos, WINDOW)
        return (fine_part, local_part)

    fine, local = lax.map(both_blocks, jnp.arange(steps, dtype=jnp.int32))
    fine = fine.reshape(toks, HEADS, HEAD_DIM)
    local = local.reshape(toks, HEADS, HEAD_DIM)
    gates = jax.nn.sigmoid(
        jnp.dot(queries, gate_weight, preferred_element_type=jnp.float32)
    ).reshape(toks, 3, HEADS)
    mixed = (
        gates[:, 0, :, None] * coarse + gates[:, 1, :, None] * fine + gates[:, 2, :, None] * local
    )
    return mixed.astype(jnp.bfloat16).reshape(toks, HEADS * HEAD_DIM)


def solution(mesh):
    return jax.shard_map(
        per_device,
        mesh=mesh,
        in_specs=(
            P(("blk", "grp"), None),
            P(("blk", "grp"), None),
            P(("blk", "grp"), None),
            P(),
            P(),
            P(),
            P(),
            P(),
            P(),
            P(),
        ),
        out_specs=P(("blk", "grp"), None),
        check_vma=False,
    )
```

profile of v0, /device:TPU:0, one launch (start us, length us, event | category | flops | bytes accessed | tf_op | source)
XLA Modules:
  0.0 162.3 jit_solution(4513411098601739997)
XLA Ops:
  0.0 3.2 %collective-permute-start = (bf16[512,128]{1,0:T(8,128)(2,1)}, bf16[512,128]{1,0:T(8,128)(2,1)}, u32[]{:S(2)}, u32[]{:S(2)}) collective-permute-start(bf16[512,128]{1,0:T(8,128)(2,1)} %param.13), channel_id=1, source_target_pairs={{0,1},{1,2},{2,3},{3,4},{4,5},{5,6},{6,7},{7,8},{8,9},{9,10},{10,1... | collective-permute-start | bytes 393224 | tf_op jit(solution)/shard_map/ppermute | solution.py:20
  3.2 4.5 %collective-permute-start.1 = (bf16[512,128]{1,0:T(8,128)(2,1)}, bf16[512,128]{1,0:T(8,128)(2,1)}, u32[]{:S(2)}, u32[]{:S(2)}) collective-permute-start(bf16[512,128]{1,0:T(8,128)(2,1)} %param.14), channel_id=1, source_target_pairs={{0,1},{1,2},{2,3},{3,4},{4,5},{5,6},{6,7},{7,8},{8,9},{9,10},{10,1... | collective-permute-start | bytes 393224 | tf_op jit(solution)/shard_map/ppermute | solution.py:20
  7.7 6.7 %all_gather.12 = bf16[2048,128]{1,0:T(8,128)(2,1)S(1)} all-gather(bf16[512,128]{1,0:T(8,128)(2,1)} %param.13), channel_id=1, replica_groups=mesh['blk'=8,'grp'=4] {'grp'}, dimensions={0}, use_global_device_ids=true | all-gather | bytes 655360 | tf_op jit(solution)/shard_map/all_gather | solution.py:121
  14.4 7.5 %all_gather.14 = bf16[2048,128]{1,0:T(8,128)(2,1)S(1)} all-gather(bf16[512,128]{1,0:T(8,128)(2,1)} %param.14), channel_id=1, replica_groups=mesh['blk'=8,'grp'=4] {'grp'}, dimensions={0}, use_global_device_ids=true | all-gather | bytes 655360 | tf_op jit(solution)/shard_map/all_gather | solution.py:122
  22.9 1.1 pad_maximum_fusion
  24.0 1.8 %gather_fusion.1 = bf16[8,64,256]{2,1,0:T(8,128)(2,1)S(1)} fusion(bf16[32,64,256]{2,1,0:T(8,128)(2,1)} %bitcast.141, s32[1024]{0:T(1024)S(1)} %pad_clamp_fusion.1), kind=kCustom, calls=%fused_computation.1 | custom fusion | bytes 524320 | tf_op jit(solution)/shard_map/jit(_take)/gather | solution.py:151
  26.6 6.0 %all-to-all-start = ((bf16[8,64,256]{2,1,0:T(8,128)(2,1)}), bf16[8,64,256]{2,1,0:T(8,128)(2,1)S(1)}, u32[]{:S(2)}, u32[]{:S(2)}) async-start(bf16[8,64,256]{2,1,0:T(8,128)(2,1)} %broadcast_select_fusion), calls=%async_computation | async-start | bytes 524288 | tf_op jit(solution)/shard_map/all_to_all | solution.py:152
  33.2 1.2 reshape.482
  34.4 1.2 reshape.485
  38.1 1.8 %convolution_convert_fusion.1 = bf16[64,128]{1,0:T(8,128)(2,1)S(1)} fusion(bf16[256,128]{1,0:T(8,128)(2,1)S(1)} %copy-done.9, bf16[4096,256]{1,0:T(8,128)(2,1)S(1)} %copy-done, f32[64,4096]{1,0:T(8,128)} %reshape.482, f32[4096]{0:T(1024)S(1)} %get-tuple-element.393), kind=kOutput, calls=%fused_computation.58 | convolution fusion | flops 139026432 | bytes 3244032 | tf_op jit(solution)/shard_map/dot_general | solution.py:33
  39.9 31.1 %all_gather.13 = bf16[512,128]{1,0:T(8,128)(2,1)S(1)} all-gather(bf16[64,128]{1,0:T(8,128)(2,1)S(1)} %convolution_convert_fusion.1), channel_id=1, replica_groups=mesh['blk'=8,'grp'=4] {'blk'}, dimensions={0}, use_global_device_ids=true | all-gather | bytes 147456 | tf_op jit(solution)/shard_map/all_gather | solution.py:137
  71.2 0.9 broadcast_compare_fusion.2
  73.0 0.9 fusion.30
  73.9 1.0 copy-done.1
  74.9 2.5 %convolution_convert_fusion = bf16[64,128]{1,0:T(8,128)(2,1)S(1)} fusion(bf16[256,128]{1,0:T(8,128)(2,1)S(1)} %copy-done.10, bf16[4096,256]{1,0:T(8,128)(2,1)} %param.18, f32[64,4096]{1,0:T(8,128)} %reshape.485, f32[4096]{0:T(1024)S(1)} %get-tuple-element.392), kind=kOutput, calls=%fused_computation.57 | convolution fusion | flops 139026432 | bytes 3244032 | tf_op jit(solution)/shard_map/dot_general | solution.py:33
  77.4 30.7 %all_gather.15 = bf16[512,128]{1,0:T(8,128)(2,1)S(1)} all-gather(bf16[64,128]{1,0:T(8,128)(2,1)S(1)} %convolution_convert_fusion), channel_id=1, replica_groups=mesh['blk'=8,'grp'=4] {'blk'}, dimensions={0}, use_global_device_ids=true | all-gather | bytes 147456 | tf_op jit(solution)/shard_map/all_gather | solution.py:138
  108.1 1.3 fusion.41
  109.5 4.3 %divide_multiply_fusion = f32[512,4,128]{0,2,1:T(8,128)} fusion(f32[512,512,4]{1,0,2:T(8,128)} %copy-done.1, f32[512,4]{0,1:T(4,128)S(1)} %broadcast_maximum_fusion, pred[512,512]{0,1:T(8,128)(4,1)S(1)} %broadcast_compare_fusion.2, f32[512,4]{0,1:T(4,128)S(1)} %get-tuple-element.395, f32[512,4]{0,1:T(4,128)S(1)} %get-tuple-element.394, ...), kind=kOutput, calls=%fused_computation.65 | convolution fusion | flops 273416192 | bytes 5668864 | tf_op jit(solution)/shard_map/while/body/eval_jaxpr/qhk,kd->qhd/dot_general | solution.py:83
  113.9 2.6 %copy.24 = f32[512,512]{1,0:T(8,128)} copy(f32[512,512]{0,1:T(8,128)} %bitcast.143) | data formatting | bytes 2097152 | tf_op jit(solution)/shard_map/mul | solution.py:194
  116.5 2.6 %gather_fusion = bf16[16,64,256]{2,1,0:T(8,128)(2,1)} fusion(bf16[32,64,256]{2,1,0:T(8,128)(2,1)} %bitcast.142, s32[1024]{0:T(1024)S(1)} %get-tuple-element.402), kind=kCustom, calls=%fused_computation | custom fusion | bytes 1048640 | tf_op jit(solution)/shard_map/jit(_take)/gather | solution.py:155
  121.4 0.9 pad_maximum_fusion.1
  122.3 1.6 %pad_maximum_fusion.2 = bf16[1024,128]{1,0:T(8,128)(2,1)} fusion(bf16[512,128]{1,0:T(8,128)(2,1)S(1)} %copy-done.6, bf16[512,128]{1,0:T(8,128)(2,1)} %collective-permute-done.1), kind=kLoop, calls=%fused_computation.77 | loop fusion | flops 524288 | bytes 524288 | tf_op jit(solution)/shard_map/concatenate | solution.py:170
  124.0 1.4 gather_fusion.2
  125.3 1.9 %fusion.49 = bf16[1024,256]{1,0:T(8,128)(2,1)S(1)} fusion(bf16[16,64,256]{2,1,0:T(8,128)(2,1)} %gather_fusion.2, bf16[16,64,256]{2,1,0:T(8,128)(2,1)} %gather_fusion, pred[1024]{0:T(1024)(128)(4,1)S(1)} %broadcast_in_dim.198, pred[1024]{0:T(1024)(128)(4,1)S(1)} %broadcast_in_dim.194, pred[1024]{0:T(1024)(128)(4,1)S(1)} %broadcast_in_dim.191), kind=kLoop, calls=%fused_computation.71 | loop fusion | flops 786432 | bytes 1575936 | tf_op jit(solution)/shard_map/jit(_where)/select_n | solution.py:157
  127.9 28.5 %while.24 = (s32[]{:T(128)}, f32[4,128,4,128]{3,2,1,0:T(4,128)}, f32[4,128,4,128]{3,2,1,0:T(4,128)}, s32[4]{0:T(128)S(1)}, s32[512]{0:T(512)}, /*index=5*/bf16[5...) while((s32[]{:T(128)}, f32[4,128,4,128]{3,2,1,0:T(4,128)}, ...), condition=%wide.region_8.9_spmd.clone, body=%wide.region_3.8_spmd.clone.sunk | while | flops 445252480 | bytes 15753344 | solution.py:187
  133.9 1.2 copy_dynamic-update-slice_fusion.3
  141.0 1.1 copy_dynamic-update-slice_fusion.3
  148.2 1.2 copy_dynamic-update-slice_fusion.3
  155.3 1.1 copy_dynamic-update-slice_fusion.3
  156.5 1.7 %mul.142 = f32[512,4,128]{2,1,0:T(4,128)S(1)} broadcast(f32[512,4]{1,0:T(8,128)} %copy.20), dimensions={0,1} | broadcast | bytes 1056768 | tf_op jit(solution)/shard_map/mul | solution.py:194
  158.2 1.6 mul.147
  159.7 2.5 %fusion.43 = bf16[512,512]{1,0:T(8,128)(2,1)} fusion(f32[64,8,4,128]{3,2,1,0:T(4,128)} %bitcast.145, f32[64,8,4,128]{3,2,1,0:T(4,128)S(1)} %bitcast.140, f32[512,512]{1,0:T(8,128)S(1)} %copy-done.2, f32[64,8,4,128]{3,2,1,0:T(4,128)S(1)} %bitcast.144, f32[64,8,4,128]{3,2,1,0:T(4,128)S(1)} %bitcast.139), kind=kLoop, calls=%fused_computation.61 | loop fusion | flops 1310720 | bytes 5767168 | tf_op jit(solution)/shard_map/convert_element_type | solution.py:196
  (150 shorter events, 29.8 us)
Async XLA Ops:
  0.0 38.1 %copy-start = (bf16[4096,256]{1,0:T(8,128)(2,1)S(1)}, bf16[4096,256]{1,0:T(8,128)(2,1)}, u32[]{:S(2)}) copy-start(bf16[4096,256]{1,0:T(8,128)(2,1)} %param.16) | copy-start | bytes 6291460
  0.0 121.4 %collective-permute-start = (bf16[512,128]{1,0:T(8,128)(2,1)}, bf16[512,128]{1,0:T(8,128)(2,1)}, u32[]{:S(2)}, u32[]{:S(2)}) collective-permute-start(bf16[512,128]{1,0:T(8,128)(2,1)} %param.13), channel_id=1, source_target_pairs={{0,1},{1,2},{2,3},{3,4},{4,5},{5,6},{6,7},{7,8},{8,9},{9,10},{10,1... | collective-permute-start | bytes 393224 | tf_op jit(solution)/shard_map/ppermute | solution.py:20
  3.2 119.1 %collective-permute-start.1 = (bf16[512,128]{1,0:T(8,128)(2,1)}, bf16[512,128]{1,0:T(8,128)(2,1)}, u32[]{:S(2)}, u32[]{:S(2)}) collective-permute-start(bf16[512,128]{1,0:T(8,128)(2,1)} %param.14), channel_id=1, source_target_pairs={{0,1},{1,2},{2,3},{3,4},{4,5},{5,6},{6,7},{7,8},{8,9},{9,10},{10,1... | collective-permute-start | bytes 393224 | tf_op jit(solution)/shard_map/ppermute | solution.py:20
  25.8 9.8 %copy-start.11 = (s32[32,16]{0,1:T(8,128)S(1)}, s32[32,16]{0,1:T(8,128)}, u32[]{:S(2)}) copy-start(s32[32,16]{0,1:T(8,128)} %param.15) | copy-start | bytes 6148
  25.8 12.3 %copy-start.12 = (bf16[2,32,128]{2,1,0:T(8,128)(2,1)S(1)}, bf16[2,32,128]{2,1,0:T(8,128)(2,1)}, u32[]{:S(2)}) copy-start(bf16[2,32,128]{2,1,0:T(8,128)(2,1)} %param.20) | copy-start | bytes 49156
  25.8 12.3 %copy-start.9 = (bf16[256,128]{1,0:T(8,128)(2,1)S(1)}, bf16[256,128]{1,0:T(8,128)(2,1)}, u32[]{:S(2)}) copy-start(bf16[256,128]{1,0:T(8,128)(2,1)} %param.17) | copy-start | bytes 196612
  26.6 97.4 %all-to-all-start = ((bf16[8,64,256]{2,1,0:T(8,128)(2,1)}), bf16[8,64,256]{2,1,0:T(8,128)(2,1)S(1)}, u32[]{:S(2)}, u32[]{:S(2)}) async-start(bf16[8,64,256]{2,1,0:T(8,128)(2,1)} %broadcast_select_fusion), calls=%async_computation | async-start | bytes 524288 | tf_op jit(solution)/shard_map/all_to_all | solution.py:152
  35.6 35.4 %copy-start.3 = (bf16[512,512]{1,0:T(8,128)(2,1)S(1)}, bf16[512,512]{1,0:T(8,128)(2,1)}, u32[]{:S(2)}) copy-start(bf16[512,512]{1,0:T(8,128)(2,1)} %param.12) | copy-start | bytes 1572868
  73.0 1.9 %copy-start.1 = (f32[512,512,4]{1,0,2:T(8,128)}, f32[512,512,4]{1,0,2:T(8,128)S(1)}, u32[]{:S(2)}) copy-start(f32[512,512,4]{1,0,2:T(8,128)S(1)} %get-tuple-element.400) | copy-start | bytes 12582916
  73.0 1.9 %copy-start.10 = (bf16[256,128]{1,0:T(8,128)(2,1)S(1)}, bf16[256,128]{1,0:T(8,128)(2,1)}, u32[]{:S(2)}) copy-start(bf16[256,128]{1,0:T(8,128)(2,1)} %param.19) | copy-start | bytes 196612
  74.9 33.2 %copy-start.13 = (bf16[512,12]{0,1:T(8,128)(2,1)S(1)}, bf16[512,12]{0,1:T(8,128)(2,1)}, u32[]{:S(2)}) copy-start(bf16[512,12]{0,1:T(8,128)(2,1)} %param.21) | copy-start | bytes 36868
  74.9 34.6 %copy-start.19 = (s32[16]{0:T(128)S(1)}, s32[16]{0:T(128)}, u32[]{:S(2)}) copy-start(s32[16]{0:T(128)} %get-tuple-element.380) | copy-start | bytes 196
  109.5 4.4 %copy-start.17 = (s32[16]{0:T(128)S(1)}, s32[16]{0:T(128)}, u32[]{:S(2)}) copy-start(s32[16]{0:T(128)} %get-tuple-element.397) | copy-start | bytes 196
  109.5 4.4 %copy-start.18 = (s32[16]{0:T(128)S(1)}, s32[16]{0:T(128)}, u32[]{:S(2)}) copy-start(s32[16]{0:T(128)} %get-tuple-element.398) | copy-start | bytes 196
  113.9 5.4 %copy-start.16 = (pred[16]{0:T(512)(128)(4,1)S(1)}, pred[16]{0:T(512)(128)(4,1)}, u32[]{:S(2)}) copy-start(pred[16]{0:T(512)(128)(4,1)} %get-tuple-element.379) | copy-start | bytes 52
  113.9 5.6 %copy-start.15 = (pred[16]{0:T(512)(128)(4,1)S(1)}, pred[16]{0:T(512)(128)(4,1)}, u32[]{:S(2)}) copy-start(pred[16]{0:T(512)(128)(4,1)} %get-tuple-element.396) | copy-start | bytes 52
  113.9 7.5 %copy-start.5 = (bf16[512,128]{1,0:T(8,128)(2,1)S(1)}, bf16[512,128]{1,0:T(8,128)(2,1)}, u32[]{:S(2)}) copy-start(bf16[512,128]{1,0:T(8,128)(2,1)} %param.13) | copy-start | bytes 393220
  113.9 8.4 %copy-start.6 = (bf16[512,128]{1,0:T(8,128)(2,1)S(1)}, bf16[512,128]{1,0:T(8,128)(2,1)}, u32[]{:S(2)}) copy-start(bf16[512,128]{1,0:T(8,128)(2,1)} %param.14) | copy-start | bytes 393220
  122.3 5.6 %copy-start.14 = (s32[16]{0:T(128)S(1)}, s32[16]{0:T(128)}, u32[]{:S(2)}) copy-start(s32[16]{0:T(128)} %broadcast_multiply_fusion) | copy-start | bytes 196
  130.4 1.2 copy-start.8
  132.3 1.1 copy-start.7
  137.5 1.2 copy-start.8
  139.5 1.1 copy-start.7
  144.7 1.2 copy-start.8
  146.6 1.1 copy-start.7
  151.8 1.2 copy-start.8
  153.7 1.1 copy-start.7
  156.5 3.3 %copy-start.2 = (f32[512,512]{1,0:T(8,128)S(1)}, f32[512,512]{1,0:T(8,128)}, u32[]{:S(2)}) copy-start(f32[512,512]{1,0:T(8,128)} %copy.24) | copy-start | bytes 3145732
  156.5 3.3 %copy-start.4 = (f32[4,128,4,128]{3,2,1,0:T(4,128)S(1)}, f32[4,128,4,128]{3,2,1,0:T(4,128)}, u32[]{:S(2)}) copy-start(f32[4,128,4,128]{3,2,1,0:T(4,128)} %get-tuple-element.299) | copy-start | bytes 3145732
where the time goes:
time: 163 us; the launch traced here: 162 us
  blocking collectives  76 us (47%)
  local copies, waits for them, and re-layouts  26.9 us (17%)
  other arithmetic  22.7 us (14%)
  matrix products  19.6 us (12%)
  starting transfers between devices  13.7 us (8%)
  loops' own time  3.12 us (2%)
    all_gather x1, blocking collectives, per_device(): lax.all_gather(packed[0], 'blk', axis=0, tiled=True)  31.1 us
    all_gather x1, blocking collectives, per_device(): lax.all_gather(packed[1], 'blk', axis=0, tiled=True)  30.7 us
    ppermute x2, starting transfers between devices, from_behind(): return lax.ppermute(block, axis, route)  7.7 us
    all_gather x1, blocking collectives, per_device(): lax.all_gather(values, 'grp', axis=0, tiled=True)  7.48 us
    all_gather x1, blocking collectives, per_device(): lax.all_gather(keys, 'grp', axis=0, tiled=True)  6.7 us
    all_to_all x1, starting transfers between devices, per_device(): lax.all_to_all(outgoing, 'blk', split_axis=0, concat_axis=0, tiled=True)  6 us
    dynamic_update_slice x4, local copies, waits for them, and re-layouts, per_device(): fine, local = lax.map(both_blocks, jnp.arange(steps, dtype=jnp.int32))  4.64 us
    dot_general x8, matrix products, attend(): jnp.einsum('qhd,kd->qhk', query_rows, key_rows, preferred_element_type=jn...  4.55 us
  transfers between devices with their start and end apart: 3, of which 0 were waited for; matrix products, arithmetic and copies ran while one was open for 20% of the time, Pallas kernels for 0%

commit v1 on v0

v1 whole, which is shorter than its diff:
```python
import functools
import math

import jax
import jax.numpy as jnp
from jax import lax
from jax.experimental import pallas as pl
from jax.experimental.pallas import tpu as pltpu
from jax.sharding import PartitionSpec as P

HEAD_DIM = 128
HEADS = 4
CMP_BLOCK = 32
SEL_BLOCK = 64
TOPN = 16
WINDOW = 512
ROWS = 128

NEG = -1e30
RATE = HEAD_DIM**-0.5 * math.log2(math.e)
MESH = pl.DeviceIdType.MESH
F32 = jnp.float32
BF16 = jnp.bfloat16


def across(a, b):
    return lax.dot_general(a, b, (((1,), (1,)), ((), ())), preferred_element_type=F32)


def branch(parts, value_parts, floor):
    top = functools.reduce(jnp.maximum, [jnp.max(s, axis=0, keepdims=True) for s in parts])
    total = 0.0
    if floor:
        top = jnp.maximum(top, 0.0)
        total = jnp.exp2(-top * RATE)
    mixed = 0.0
    for s, v in zip(parts, value_parts):
        weights = jnp.exp2((s - top) * RATE)
        total = total + jnp.sum(weights, axis=0, keepdims=True)
        mixed = mixed + jnp.dot(v, weights.astype(BF16), preferred_element_type=F32)
    return mixed, total


def kernel(
    B,
    G,
    sel,
    queries,
    keys,
    values,
    key_in,
    key_out,
    value_in,
    value_out,
    positions,
    gate_weight,
    out,
    w_in,
    w_out,
    shifted,
    sk,
    sv,
    pk,
    pv,
    ik,
    iv,
    stk,
    stv,
    cc,
    cvt,
    wk,
    wvt,
    fk,
    fv,
    fvt,
    pool,
    acc,
    gates,
    w_sem,
    a_s,
    a_r,
    m_s,
    m_r,
    p_s,
    p_r,
    b_s,
    b_r,
    c_s,
    c_r,
    f_s,
    f_r,
):
    T = keys.shape[0] * SEL_BLOCK
    N = T // CMP_BLOCK
    Y = G // 2
    per_row = G * T // SEL_BLOCK
    b = lax.axis_index("blk")
    g = lax.axis_index("grp")
    y = g // 2
    core = g % 2
    mate = g + 1 - 2 * core
    position = b * G + g
    first = position * T

    loads = [
        pltpu.make_async_copy(src, dst, w_sem.at[n])
        for n, (src, dst) in enumerate(
            (
                (key_in, w_in.at[0]),
                (value_in, w_in.at[1]),
                (key_out, w_out.at[0]),
                (value_out, w_out.at[1]),
            )
        )
    ]
    for load in loads:
        load.start()

    cc[...] = jnp.zeros_like(cc)
    pk[...] = jnp.zeros_like(pk)
    pv[...] = jnp.zeros_like(pv)

    def remote(src, dst, send, recv, dev):
        return pltpu.make_async_remote_copy(
            src_ref=src,
            dst_ref=dst,
            send_sem=send,
            recv_sem=recv,
            device_id=dev,
            device_id_type=MESH,
        )

    def at(stretch, column):
        return {"blk": stretch, "grp": column}

    last = jnp.logical_and(g == G - 1, b < B - 1)
    head = jnp.logical_and(g == 0, b > 0)
    barrier = pltpu.get_barrier_semaphore()

    def greet(dev):
        pl.semaphore_signal(barrier, inc=1, device_id=dev, device_id_type=MESH)

    for e in range(1, G):
        greet(at(b, (g + e) % G))
    for d in range(1, B):
        greet(at((b + d) % B, g))

    @pl.when(last)
    def _():
        greet(at(b + 1, 0))

    @pl.when(head)
    def _():
        greet(at(b - 1, G - 1))

    here = pl.ds(g * (T // SEL_BLOCK), T // SEL_BLOCK)
    sk[here] = keys[...]
    sv[here] = values[...]
    pl.semaphore_wait(barrier, G - 1 + B - 1 + last.astype(jnp.int32) + head.astype(jnp.int32))

    own = (keys, values)
    row = (sk, sv)
    prev = (pk, pv)
    staged = (stk, stv)
    inbox = (ik, iv)

    def slot(column):
        return pl.ds(column * (T // SEL_BLOCK), T // SEL_BLOCK)

    def over_y(c, e):
        return remote(
            own[c], row[c].at[slot(g)], a_s.at[c, e], a_r.at[c, e], at(b, ((y + e) % Y) * 2 + core)
        )

    def to_mate(c, e):
        source = ((y - e + Y) % Y) * 2 + core
        src = own[c] if e == 0 else row[c].at[slot(source)]
        return remote(src, row[c].at[slot(source)], m_s.at[c, e], m_r.at[c, e], at(b, mate))

    def to_next(c):
        return remote(own[c], prev[c], p_s.at[c], p_r.at[c], at((b + 1) % B, 0))

    def block_out(c, d):
        return remote(
            staged[c].at[d - 1], inbox[c].at[b], b_s.at[c, d], b_r.at[c, d], at((b + d) % B, g)
        )

    def coarse_out(d):
        part = cc.at[g, :, pl.ds(pl.multiple_of(b * N, N), N), :]
        return remote(part, part, c_s.at[d], c_r.at[d], at((b + d) % B, g))

    def coarse_share(e):
        return remote(cc.at[g], cc.at[g], f_s.at[e], f_r.at[e], at(b, (g + e) % G))

    for c in range(2):
        for e in range(1, Y):
            over_y(c, e).start()
        to_mate(c, 0).start()

        @pl.when(last)
        def _(c=c):
            to_next(c).start()

    for c in range(2):
        shift = positions[c].astype(F32)
        shifted[c] = (
            own[c][...].astype(F32).reshape(N, CMP_BLOCK, HEAD_DIM) + shift[None]
        ).reshape(T, HEAD_DIM)
    for load in loads:
        load.wait()
    mine_rows = pl.ds(pl.multiple_of(b * N, N), N)
    for c in range(2):
        flat = jnp.concatenate(
            [shifted[c, pl.ds(t, N, stride=CMP_BLOCK), :].astype(BF16) for t in range(CMP_BLOCK)],
            axis=1,
        )
        hidden = jax.nn.silu(jnp.dot(flat, w_in[c], preferred_element_type=F32)).astype(BF16)
        cc[g, c, mine_rows, :] = jnp.dot(hidden, w_out[c], preferred_element_type=F32).astype(BF16)
    for d in range(1, B):

        @pl.when(b + d < B)
        def _(d=d):
            coarse_out(d).start()

    def home(j):
        owner = lax.div(j, per_row)
        return owner, j - owner * per_row

    def same(left, right):
        gap = left - right
        return 1 - jnp.minimum(jnp.maximum(gap, -gap), 1)

    picks = []
    for d in range(1, B):
        line = jnp.minimum(b + d, B - 1) * G + g
        pick = jnp.int32(0)
        for i in range(TOPN):
            owner, rank = home(sel[line, i])
            pick = pick + same(owner, b) * rank
        picks.append(pick)

    gates[...] = jax.nn.sigmoid(
        lax.dot_general(
            gate_weight[...], queries[...], (((0,), (1,)), ((), ())), preferred_element_type=F32
        )
    )

    for c in range(2):
        for e in range(1, Y):
            over_y(c, e).wait_recv()
            to_mate(c, e).start()
        for e in range(Y):
            to_mate(c, e).wait_recv()
        for d in range(1, B):

            @pl.when(b + d < B)
            def _(c=c, d=d):
                staged[c][d - 1] = row[c][picks[d - 1]]

        for d in range(1, B):

            @pl.when(b + d < B)
            def _(c=c, d=d):
                block_out(c, d).start()

    for d in range(1, B):

        @pl.when(b - d >= 0)
        def _(d=d):
            coarse_out(d).wait_recv()

    for e in range(1, G):
        coarse_share(e).start()

    @pl.when(head)
    def _():
        for c in range(2):
            to_next(c).wait_recv()

    before = slot(jnp.maximum(g - 1, 0))
    flat = (T, HEAD_DIM)
    wk[pl.ds(0, T), :] = jnp.where(g == 0, pk[...], sk[before]).reshape(flat)
    wk[pl.ds(T, T), :] = keys[...].reshape(flat)
    wvt[:, pl.ds(0, T)] = jnp.where(g == 0, pv[...], sv[before]).reshape(flat).T
    wvt[:, pl.ds(T, T)] = values[...].reshape(flat).T

    lanes = HEADS * ROWS

    def query_block(start):
        rows = queries[pl.ds(start, ROWS), :]
        return jnp.concatenate(
            [rows[:, h * HEAD_DIM : (h + 1) * HEAD_DIM] for h in range(HEADS)], axis=0
        )

    def gate(n, start):
        return jnp.concatenate(
            [gates[n * HEADS + h : n * HEADS + h + 1, pl.ds(start, ROWS)] for h in range(HEADS)],
            axis=1,
        )

    def iotas(count):
        k = lax.broadcasted_iota(jnp.int32, (count, lanes), 0)
        q = lax.broadcasted_iota(jnp.int32, (count, lanes), 1) % ROWS
        return k, q

    def window_step(step, carry):
        start = pl.multiple_of(step * ROWS, ROWS)
        span = pl.ds(pl.multiple_of(start + T - WINDOW, ROWS), ROWS + WINDOW)
        s = across(wk[span, :], query_block(start))
        k, q = iotas(ROWS)
        opening = jnp.where(position == 0, WINDOW - start, 0)
        kk = lax.broadcasted_iota(jnp.int32, (WINDOW - ROWS, lanes), 0) + ROWS
        parts = [
            jnp.where((k > q) & (k >= opening), s[:ROWS], NEG),
            jnp.where(kk >= opening, s[ROWS:WINDOW], NEG),
            jnp.where(k <= q, s[WINDOW:], NEG),
        ]
        vt = wvt[:, span]
        mixed, total = branch(parts, [vt[:, :ROWS], vt[:, ROWS:WINDOW], vt[:, WINDOW:]], False)
        acc[step] = mixed * (gate(2, start) / total)
        return carry

    lax.fori_loop(0, T // ROWS, window_step, 0)

    for e in range(1, G):
        coarse_share(e).wait_recv()
    for column in range(G):
        cvt[:, pl.ds(column * B * N, B * N)] = cc[column, 1].T

    def coarse_step(step, carry):
        start = pl.multiple_of(step * ROWS, ROWS)
        query = query_block(start)
        k, q = iotas(B * N)
        end = (k // N) * (G * T) + (k % N) * CMP_BLOCK + CMP_BLOCK - 1 - q
        parts = []
        for column in range(G):
            s = across(cc[column, 0], query)
            parts.append(jnp.where(end <= first + start - column * T, s, NEG))
        vts = [cvt[:, pl.ds(column * B * N, B * N)] for column in range(G)]
        mixed, total = branch(parts, vts, True)
        acc[step] = acc[step] + mixed * (gate(0, start) / total)
        return carry

    lax.fori_loop(0, T // ROWS, coarse_step, 0)

    for c in range(2):
        for d in range(1, B):

            @pl.when(b - d >= 0)
            def _(c=c, d=d):
                block_out(c, d).wait_recv()

    for c in range(2):
        pool[c, :per_row] = row[c][...]
        pool[c, per_row:] = inbox[c][...]
    starts = []
    for i in range(TOPN):
        j = sel[position, i]
        owner, rank = home(j)
        near = same(owner, b)
        entry = near * rank + (1 - near) * (per_row + owner)
        starts.append(j * SEL_BLOCK)
        for c, into in ((0, fk), (1, fv)):
            into[pl.ds(i * SEL_BLOCK, SEL_BLOCK), :] = pool[c, entry]
    fvt[...] = fv[...].T

    def fine_step(step, carry):
        start = pl.multiple_of(step * ROWS, ROWS)
        s = across(fk[...], query_block(start))
        k, q = iotas(SEL_BLOCK)
        ahead = k - q
        parts = [
            jnp.where(
                ahead <= first + start - starts[i], s[i * SEL_BLOCK : (i + 1) * SEL_BLOCK], NEG
            )
            for i in range(TOPN)
        ]
        s = jnp.concatenate(parts, axis=0)
        mixed, total = branch([s], [fvt[...]], False)
        mixed = acc[step] + mixed * (gate(1, start) / total)
        for h in range(HEADS):
            out[pl.ds(start, ROWS), h * HEAD_DIM : (h + 1) * HEAD_DIM] = mixed[
                :, h * ROWS : (h + 1) * ROWS
            ].T.astype(BF16)
        return carry

    lax.fori_loop(0, T // ROWS, fine_step, 0)

    for c in range(2):
        for e in range(1, Y):
            over_y(c, e).wait_send()
        for e in range(Y):
            to_mate(c, e).wait_send()

        @pl.when(last)
        def _(c=c):
            to_next(c).wait_send()

        for d in range(1, B):

            @pl.when(b + d < B)
            def _(c=c, d=d):
                block_out(c, d).wait_send()

    for d in range(1, B):

        @pl.when(b + d < B)
        def _(d=d):
            coarse_out(d).wait_send()

    for e in range(1, G):
        coarse_share(e).wait_send()


def per_device(
    queries, keys, values, selected, key_in, key_out, value_in, value_out, positions, gate_weight
):
    B = lax.axis_size("blk")
    G = lax.axis_size("grp")
    T = keys.shape[0]
    N = T // CMP_BLOCK
    Y = G // 2
    inner, hidden = key_in.shape
    vmem = pl.BlockSpec(memory_space=pltpu.VMEM)
    smem = pl.BlockSpec(memory_space=pltpu.SMEM)
    hbm = pl.BlockSpec(memory_space=pl.ANY)
    dma = pltpu.SemaphoreType.DMA

    def buf(*shape, dtype=BF16):
        return pltpu.VMEM(shape, dtype)

    return pl.pallas_call(
        functools.partial(kernel, B, G),
        out_shape=jax.ShapeDtypeStruct(queries.shape, BF16),
        in_specs=[smem, vmem, vmem, vmem, hbm, hbm, hbm, hbm, vmem, vmem],
        out_specs=vmem,
        scratch_shapes=[
            buf(2, inner, hidden),
            buf(2, hidden, HEAD_DIM),
            buf(2, T, HEAD_DIM, dtype=F32),
            buf(G * T // SEL_BLOCK, SEL_BLOCK, HEAD_DIM),
            buf(G * T // SEL_BLOCK, SEL_BLOCK, HEAD_DIM),
            buf(T // SEL_BLOCK, SEL_BLOCK, HEAD_DIM),
            buf(T // SEL_BLOCK, SEL_BLOCK, HEAD_DIM),
            buf(B, SEL_BLOCK, HEAD_DIM),
            buf(B, SEL_BLOCK, HEAD_DIM),
            buf(B - 1, SEL_BLOCK, HEAD_DIM),
            buf(B - 1, SEL_BLOCK, HEAD_DIM),
            buf(G, 2, B * N, HEAD_DIM),
            buf(HEAD_DIM, G * B * N),
            buf(2 * T, HEAD_DIM),
            buf(HEAD_DIM, 2 * T),
            buf(TOPN * SEL_BLOCK, HEAD_DIM),
            buf(TOPN * SEL_BLOCK, HEAD_DIM),
            buf(HEAD_DIM, TOPN * SEL_BLOCK),
            buf(2, G * T // SEL_BLOCK + B, SEL_BLOCK, HEAD_DIM),
            buf(T // ROWS, HEAD_DIM, HEADS * ROWS, dtype=F32),
            buf(3 * HEADS, T, dtype=F32),
            dma((4,)),
            dma((2, Y)),
            dma((2, Y)),
            dma((2, Y)),
            dma((2, Y)),
            dma((2,)),
            dma((2,)),
            dma((2, B)),
            dma((2, B)),
            dma((B,)),
            dma((B,)),
            dma((G,)),
            dma((G,)),
        ],
        compiler_params=pltpu.CompilerParams(
            collective_id=0, has_side_effects=True, vmem_limit_bytes=56 << 20
        ),
    )(
        selected,
        queries,
        keys.reshape(T // SEL_BLOCK, SEL_BLOCK, HEAD_DIM),
        values.reshape(T // SEL_BLOCK, SEL_BLOCK, HEAD_DIM),
        key_in,
        key_out,
        value_in,
        value_out,
        positions,
        gate_weight,
    )


def solution(mesh):
    rows = P(("blk", "grp"), None)
    return jax.shard_map(
        per_device,
        mesh=mesh,
        in_specs=(rows, rows, rows, P(), P(), P(), P(), P(), P(), P()),
        out_specs=rows,
        check_vma=False,
    )
```

time: 163 us -> 34.8 us (0.21)
  the two profiles are of different devices: /device:TPU:0 before, /device:TPU:7 now
where the time goes in v1:
time: 34.8 us; the launch traced here: 34.5 us
  Pallas kernels  29.7 us (85%)
  local copies, waits for them, and re-layouts  4.74 us (14%)
    pallas_call x1, Pallas kernels, per_device(): pl.pallas_call(functools.partial(kernel, B, G), out_shape=jax.ShapeDtypeS...  29.7 us
    unnamed x3, local copies, waits for them, and re-layouts  4.74 us

profile of v1, /device:TPU:7, one launch (start us, length us, event | category | flops | bytes accessed | tf_op | source)
XLA Modules:
  0.0 34.5 jit_solution(10876692297304470870)
XLA Ops:
  0.0 1.4 %copy.11.sel = s32[32,16]{1,0:T(8,128)} copy(s32[32,16]{0,1:T(8,128)} %param.13) | data formatting | bytes 4096 | tf_op args[3]
  1.4 1.5 %copy.12.gate_weight = bf16[512,12]{1,0:T(8,128)(2,1)} copy(bf16[512,12]{0,1:T(8,128)(2,1)} %param.19) | data formatting | bytes 24576 | tf_op args[9]
  2.9 29.7 %shard_map.100 = bf16[512,512]{1,0:T(8,128)(2,1)} custom-call(s32[32,16]{1,0:T(8,128)} %copy.11.sel, bf16[512,512]{1,0:T(8,128)(2,1)} %queries.1, bf16[8,64,128]{2,1,0:T(8,128)(2,1)} %bitcast.2, bf16[8,64,128]{2,1,0:T(8,128)(2,1)} %bitcast.3, bf16[4096,256]{1,0:T(8,128)(2,1)} %key_in.1, bf16[256,128]{1,0:T(8,128)(2,1)} %key_out.1, ...), custom_call_target="tpu_custom_call" | custom-call | tf_op jit(solution)/shard_map/pallas_call | solution.py:432
  32.6 1.9 %copy.14 = bf16[512,512]{1,0:T(8,128)(2,1)} copy(bf16[512,512]{1,0:T(8,128)(2,1)} %shard_map.100) | data formatting | bytes 1048576

commit v2 on v1

--- a/solution.py
+++ b/solution.py
@@ -73,6 +73,7 @@
     fk,
     fv,
     fvt,
+    ends,
     pool,
     acc,
     gates,
@@ -133,7 +134,7 @@
     def at(stretch, column):
         return {"blk": stretch, "grp": column}
 
-    last = jnp.logical_and(g == G - 1, b < B - 1)
+    last = jnp.logical_and(g == 0, b < B - 1)
     head = jnp.logical_and(g == 0, b > 0)
     barrier = pltpu.get_barrier_semaphore()
 
@@ -145,18 +146,33 @@
     for d in range(1, B):
         greet(at((b + d) % B, g))
 
-    @pl.when(last)
-    def _():
-        greet(at(b + 1, 0))
-
-    @pl.when(head)
-    def _():
-        greet(at(b - 1, G - 1))
-
     here = pl.ds(g * (T // SEL_BLOCK), T // SEL_BLOCK)
     sk[here] = keys[...]
     sv[here] = values[...]
-    pl.semaphore_wait(barrier, G - 1 + B - 1 + last.astype(jnp.int32) + head.astype(jnp.int32))
+    def home(j):
+        owner = lax.div(j, per_row)
+        return owner, j - owner * per_row
+
+    def same(left, right):
+        gap = left - right
+        return 1 - jnp.minimum(jnp.maximum(gap, -gap), 1)
+
+    picks = []
+    for d in range(1, B):
+        line = jnp.minimum(b + d, B - 1) * G + g
+        pick = jnp.int32(0)
+        for i in range(TOPN):
+            owner, rank = home(sel[i, line])
+            pick = pick + same(owner, b) * rank
+        picks.append(pick)
+
+    gates[...] = jax.nn.sigmoid(
+        lax.dot_general(
+            gate_weight[...], queries[...], (((1,), (1,)), ((), ())), preferred_element_type=F32
+        )
+    )
+
+    pl.semaphore_wait(barrier, G - 1 + B - 1)
 
     own = (keys, values)
     row = (sk, sv)
@@ -178,7 +194,9 @@
         return remote(src, row[c].at[slot(source)], m_s.at[c, e], m_r.at[c, e], at(b, mate))
 
     def to_next(c):
-        return remote(own[c], prev[c], p_s.at[c], p_r.at[c], at((b + 1) % B, 0))
+        return remote(
+            row[c].at[slot(G - 1)], prev[c], p_s.at[c], p_r.at[c], at((b + 1) % B, 0)
+        )
 
     def block_out(c, d):
         return remote(
@@ -189,17 +207,19 @@
         part = cc.at[g, :, pl.ds(pl.multiple_of(b * N, N), N), :]
         return remote(part, part, c_s.at[d], c_r.at[d], at((b + d) % B, g))
 
-    def coarse_share(e):
-        return remote(cc.at[g], cc.at[g], f_s.at[e], f_r.at[e], at(b, (g + e) % G))
+    def coarse_over_y(e):
+        return remote(
+            cc.at[g], cc.at[g], f_s.at[0, e], f_r.at[0, e], at(b, ((y + e) % Y) * 2 + core)
+        )
+
+    def coarse_to_mate(e):
+        part = cc.at[((y - e + Y) % Y) * 2 + core]
+        return remote(part, part, f_s.at[1, e], f_r.at[1, e], at(b, mate))
 
     for c in range(2):
         for e in range(1, Y):
             over_y(c, e).start()
         to_mate(c, 0).start()
-
-        @pl.when(last)
-        def _(c=c):
-            to_next(c).start()
 
     for c in range(2):
         shift = positions[c].astype(F32)
@@ -222,33 +242,24 @@
         def _(d=d):
             coarse_out(d).start()
 
-    def home(j):
-        owner = lax.div(j, per_row)
-        return owner, j - owner * per_row
-
-    def same(left, right):
-        gap = left - right
-        return 1 - jnp.minimum(jnp.maximum(gap, -gap), 1)
-
-    picks = []
+    for e in range(1, Y):
+        over_y(0, e).wait_recv()
+        to_mate(0, e).start()
     for d in range(1, B):
-        line = jnp.minimum(b + d, B - 1) * G + g
-        pick = jnp.int32(0)
-        for i in range(TOPN):
-            owner, rank = home(sel[line, i])
-            pick = pick + same(owner, b) * rank
-        picks.append(pick)
-
-    gates[...] = jax.nn.sigmoid(
-        lax.dot_general(
-            gate_weight[...], queries[...], (((0,), (1,)), ((), ())), preferred_element_type=F32
-        )
-    )
-
-    for c in range(2):
-        for e in range(1, Y):
-            over_y(c, e).wait_recv()
-            to_mate(c, e).start()
+
+        @pl.when(b - d >= 0)
+        def _(d=d):
+            coarse_out(d).wait_recv()
+
+    for e in range(1, Y):
+        coarse_over_y(e).start()
+    coarse_to_mate(0).start()
+
+    for c in range(2):
+        if c == 1:
+            for e in range(1, Y):
+                over_y(c, e).wait_recv()
+                to_mate(c, e).start()
         for e in range(Y):
             to_mate(c, e).wait_recv()
         for d in range(1, B):
@@ -263,14 +274,54 @@
             def _(c=c, d=d):
                 block_out(c, d).start()
 
-    for d in range(1, B):
-
-        @pl.when(b - d >= 0)
-        def _(d=d):
-            coarse_out(d).wait_recv()
-
-    for e in range(1, G):
-        coarse_share(e).start()
+        @pl.when(last)
+        def _(c=c):
+            to_next(c).start()
+
+    for e in range(1, Y):
+        coarse_over_y(e).wait_recv()
+        coarse_to_mate(e).start()
+
+    lanes = HEADS * ROWS
+
+    def query_block(start):
+        rows = queries[pl.ds(start, ROWS), :]
+        return jnp.concatenate(
+            [rows[:, h * HEAD_DIM : (h + 1) * HEAD_DIM] for h in range(HEADS)], axis=0
+        )
+
+    def gate(n, start):
+        return jnp.concatenate(
+            [gates[n * HEADS + h : n * HEADS + h + 1, pl.ds(start, ROWS)] for h in range(HEADS)],
+            axis=1,
+        )
+
+    def iotas(count):
+        k = lax.broadcasted_iota(jnp.int32, (count, lanes), 0)
+        q = lax.broadcasted_iota(jnp.int32, (count, lanes), 1) % ROWS
+        return k, q
+
+    for e in range(Y):
+        coarse_to_mate(e).wait_recv()
+    for column in range(G):
+        cvt[:, pl.ds(column * B * N, B * N)] = cc[column, 1].T
+
+    k, q = iotas(B * N)
+    ends[...] = (k // N) * (G * T) + (k % N) * CMP_BLOCK + CMP_BLOCK - 1 - q
+
+    def coarse_step(step, carry):
+        start = pl.multiple_of(step * ROWS, ROWS)
+        query = query_block(start)
+        parts = []
+        for column in range(G):
+            s = across(cc[column, 0], query)
+            parts.append(jnp.where(ends[...] <= first + start - column * T, s, NEG))
+        vts = [cvt[:, pl.ds(column * B * N, B * N)] for column in range(G)]
+        mixed, total = branch(parts, vts, True)
+        acc[step] = mixed * (gate(0, start) / total)
+        return carry
+
+    lax.fori_loop(0, T // ROWS, coarse_step, 0, unroll=True)
 
     @pl.when(head)
     def _():
@@ -283,25 +334,6 @@
     wk[pl.ds(T, T), :] = keys[...].reshape(flat)
     wvt[:, pl.ds(0, T)] = jnp.where(g == 0, pv[...], sv[before]).reshape(flat).T
     wvt[:, pl.ds(T, T)] = values[...].reshape(flat).T
-
-    lanes = HEADS * ROWS
-
-    def query_block(start):
-        rows = queries[pl.ds(start, ROWS), :]
-        return jnp.concatenate(
-            [rows[:, h * HEAD_DIM : (h + 1) * HEAD_DIM] for h in range(HEADS)], axis=0
-        )
-
-    def gate(n, start):
-        return jnp.concatenate(
-            [gates[n * HEADS + h : n * HEADS + h + 1, pl.ds(start, ROWS)] for h in range(HEADS)],
-            axis=1,
-        )
-
-    def iotas(count):
-        k = lax.broadcasted_iota(jnp.int32, (count, lanes), 0)
-        q = lax.broadcasted_iota(jnp.int32, (count, lanes), 1) % ROWS
-        return k, q
 
     def window_step(step, carry):
         start = pl.multiple_of(step * ROWS, ROWS)
@@ -317,31 +349,10 @@
         ]
         vt = wvt[:, span]
         mixed, total = branch(parts, [vt[:, :ROWS], vt[:, ROWS:WINDOW], vt[:, WINDOW:]], False)
-        acc[step] = mixed * (gate(2, start) / total)
+        acc[step] = acc[step] + mixed * (gate(2, start) / total)
         return carry
 
-    lax.fori_loop(0, T // ROWS, window_step, 0)
-
-    for e in range(1, G):
-        coarse_share(e).wait_recv()
-    for column in range(G):
-        cvt[:, pl.ds(column * B * N, B * N)] = cc[column, 1].T
-
-    def coarse_step(step, carry):
-        start = pl.multiple_of(step * ROWS, ROWS)
-        query = query_block(start)
-        k, q = iotas(B * N)
-        end = (k // N) * (G * T) + (k % N) * CMP_BLOCK + CMP_BLOCK - 1 - q
-        parts = []
-        for column in range(G):
-            s = across(cc[column, 0], query)
-            parts.append(jnp.where(end <= first + start - column * T, s, NEG))
-        vts = [cvt[:, pl.ds(column * B * N, B * N)] for column in range(G)]
-        mixed, total = branch(parts, vts, True)
-        acc[step] = acc[step] + mixed * (gate(0, start) / total)
-        return carry
-
-    lax.fori_loop(0, T // ROWS, coarse_step, 0)
+    lax.fori_loop(0, T // ROWS, window_step, 0, unroll=True)
 
     for c in range(2):
         for d in range(1, B):
@@ -355,7 +366,7 @@
         pool[c, per_row:] = inbox[c][...]
     starts = []
     for i in range(TOPN):
-        j = sel[position, i]
+        j = sel[i, position]
         owner, rank = home(j)
         near = same(owner, b)
         entry = near * rank + (1 - near) * (per_row + owner)
@@ -384,7 +395,7 @@
             ].T.astype(BF16)
         return carry
 
-    lax.fori_loop(0, T // ROWS, fine_step, 0)
+    lax.fori_loop(0, T // ROWS, fine_step, 0, unroll=True)
 
     for c in range(2):
         for e in range(1, Y):
@@ -408,8 +419,10 @@
         def _(d=d):
             coarse_out(d).wait_send()
 
-    for e in range(1, G):
-        coarse_share(e).wait_send()
+    for e in range(1, Y):
+        coarse_over_y(e).wait_send()
+    for e in range(Y):
+        coarse_to_mate(e).wait_send()
 
 
 def per_device(
@@ -453,6 +466,7 @@
             buf(TOPN * SEL_BLOCK, HEAD_DIM),
             buf(TOPN * SEL_BLOCK, HEAD_DIM),
             buf(HEAD_DIM, TOPN * SEL_BLOCK),
+            buf(B * N, HEADS * ROWS, dtype=jnp.int32),
             buf(2, G * T // SEL_BLOCK + B, SEL_BLOCK, HEAD_DIM),
             buf(T // ROWS, HEAD_DIM, HEADS * ROWS, dtype=F32),
             buf(3 * HEADS, T, dtype=F32),
@@ -467,14 +481,14 @@
             dma((2, B)),
             dma((B,)),
             dma((B,)),
-            dma((G,)),
-            dma((G,)),
+            dma((2, Y)),
+            dma((2, Y)),
         ],
         compiler_params=pltpu.CompilerParams(
             collective_id=0, has_side_effects=True, vmem_limit_bytes=56 << 20
         ),
     )(
-        selected,
+        selected.T,
         queries,
         keys.reshape(T // SEL_BLOCK, SEL_BLOCK, HEAD_DIM),
         values.reshape(T // SEL_BLOCK, SEL_BLOCK, HEAD_DIM),
@@ -483,7 +497,7 @@
         value_in,
         value_out,
         positions,
-        gate_weight,
+        gate_weight.T,
     )
 
 

time: 34.8 us -> 31.5 us (0.905)
  the two profiles are of different devices: /device:TPU:7 before, /device:TPU:16 now
where the time goes in v2:
time: 31.5 us; the launch traced here: 31.3 us
  Pallas kernels  29.4 us (93%)
  local copies, waits for them, and re-layouts  1.87 us (6%)
    pallas_call x1, Pallas kernels, per_device(): pl.pallas_call(functools.partial(kernel, B, G), out_shape=jax.ShapeDtypeS...  29.4 us
    unnamed x1, local copies, waits for them, and re-layouts  1.87 us

profile of v2, /device:TPU:16, one launch (start us, length us, event | category | flops | bytes accessed | tf_op | source)
XLA Modules:
  0.0 31.3 jit_solution(5658220110780372072)
XLA Ops:
  0.0 29.4 %shard_map.100 = bf16[512,512]{1,0:T(8,128)(2,1)} custom-call(s32[16,32]{1,0:T(8,128)} %bitcast.7, bf16[512,512]{1,0:T(8,128)(2,1)} %queries.1, bf16[8,64,128]{2,1,0:T(8,128)(2,1)} %bitcast.4, bf16[8,64,128]{2,1,0:T(8,128)(2,1)} %bitcast.5, bf16[4096,256]{1,0:T(8,128)(2,1)} %key_in.1, bf16[256,128]{1,0:T(8,128)(2,1)} %key_out.1, bf16[4096,256]{1,0:T(8,128)(2,1)} %value_in.1, ...), custom_call_target="tpu_custom_call" | custom-call | tf_op jit(solution)/shard_map/pallas_call | solution.py:445
  29.4 1.9 %copy.12 = bf16[512,512]{1,0:T(8,128)(2,1)} copy(bf16[512,512]{1,0:T(8,128)(2,1)} %shard_map.100) | data formatting | bytes 1048576
